TPU v7x, 256 devices: a whole 4x4x8 slice. The times are simulated.
256 devices in a mesh: tok: 32 (over z, y), voc: 8 (over x, core).
Axes of the slice: x: 4, y: 4, z: 8, core: 2. Of those that a mesh axis runs over, the one named last changes fastest.
Arguments:
- hidden: bfloat16 [8192, 1536], P('tok'), may hold values from -1000 to 1000
- norm_gain: float32 [1536], replicated, may hold values from 0.1 to 1.9
- head_weight: bfloat16 [1536, 49152], P(None, ('tok', 'voc')), may hold values from -8 to 8
- targets: int32 [8192], P('tok'), may hold values from 0 to 49151
- lengths: int32 [32], replicated, may hold values from 1 to 256, 5120 in all
- prior_device: int32 [32], replicated, may hold values from 0 to 31, each once
- prior_row: int32 [32], replicated, may hold values from 0 to 255
Outputs:
- logprob: float32 [8192], P('tok')
- entropy: float32 [8192], P('tok')
Inputs may be any that keep to these rules, and one draw needn't show every extreme that they name: One turn's block is full, lengths[t] = 256. `prior_device`: every block index appears once.
All inputs are finite; a program needn't handle non-finite values.
Results may differ from a plain program's by a relative error of at most 0.0036.
Values may be sent and summed in bfloat16 or wider, within the bound.
A program may use at most 192 MiB of HBM per device.

v0:
```python
import jax
import jax.numpy as jnp
from jax import lax
from jax.sharding import PartitionSpec as P

epsilon = 1e-05


def select_entry(table, wanted):
    positions = jnp.arange(table.shape[0], dtype=jnp.int32)
    return jnp.sum(jnp.where(positions == wanted, table, 0))


def combine(first, second):
    largest = jnp.maximum(first[0], second[0])
    later = jnp.exp(second[0] - largest)
    return (largest, second[1] * later, second[2] * later, second[3])


def block_size(total_rows):
    for candidate in (512, 384, 256, 128):
        if total_rows % candidate == 0:
            return candidate
    return total_rows


def block_stats(states, columns, target_col):
    total_rows = states.shape[0]
    block_rows = block_size(total_rows)
    block_count = total_rows // block_rows
    column_ids = jnp.arange(columns.shape[1], dtype=jnp.int32)

    def score_block(inputs):
        state_rows, wanted = inputs
        logits = jnp.dot(state_rows, columns, preferred_element_type=jnp.float32)
        maxima = jnp.max(logits, axis=1)
        weights = jnp.exp(logits - maxima[:, None])
        totals = jnp.sum(weights, axis=1)
        moments = jnp.sum(weights * logits, axis=1)
        picked = jnp.sum(jnp.where(column_ids[None, :] == wanted[:, None], logits, 0.0), axis=1)
        return (maxima, totals, moments, picked)

    results = lax.map(
        score_block,
        (
            states.reshape(block_count, block_rows, states.shape[1]),
            target_col.reshape(block_count, block_rows),
        ),
    )
    return tuple((member.reshape(total_rows) for member in results))


def body(hidden, norm_gain, head_weight, targets, lengths, prior_device, prior_row):
    row_count = hidden.shape[0]
    col_width = head_weight.shape[1]
    tok_index = lax.axis_index("tok")
    band_index = lax.axis_index("voc")
    voc_count = lax.axis_size("voc")
    asked_row = jnp.sum(jnp.where(prior_device == tok_index, prior_row, 0))
    outgoing = lax.dynamic_slice_in_dim(hidden, asked_row, 1, 0)
    incoming = lax.all_gather(outgoing, "tok", axis=0, tiled=True)
    source = select_entry(prior_device, tok_index)
    chosen = jnp.arange(incoming.shape[0], dtype=jnp.int32) == source
    fetched = jnp.sum(
        jnp.where(chosen[:, None], incoming.astype(jnp.float32), 0.0), axis=0, keepdims=True
    )
    scored = jnp.concatenate([fetched, hidden[:-1].astype(jnp.float32)], axis=0)
    normed = (
        scored
        * lax.rsqrt(jnp.mean(scored * scored, axis=1, keepdims=True) + epsilon)
        * norm_gain[None, :]
    ).astype(jnp.bfloat16)
    owner_block = targets // col_width
    target_col = jnp.where(
        owner_block % voc_count == band_index,
        owner_block // voc_count * col_width + targets % col_width,
        -1,
    )
    zeroes = jnp.zeros((row_count,), jnp.float32)
    initial = (jnp.full((row_count,), -1e30, jnp.float32), zeroes, zeroes, zeroes)
    maxima, totals, moments, picked = combine(
        initial,
        block_stats(normed, lax.all_gather(head_weight, "tok", axis=1, tiled=True), target_col),
    )
    largest = lax.pmax(maxima, "voc")
    factor = jnp.exp(maxima - largest)
    totals, moments, picked = lax.psum((totals * factor, moments * factor, picked), "voc")
    maxima = largest
    normalizer = maxima + jnp.log(totals)
    logprob = picked - normalizer
    entropy = normalizer - moments / totals
    live_count = select_entry(lengths, tok_index)
    valid = jnp.arange(row_count, dtype=jnp.int32) < live_count
    return (jnp.where(valid, logprob, 0.0), jnp.where(valid, entropy, 0.0))


def solution(mesh):
    in_specs = (P("tok", None), P(), P(None, ("tok", "voc")), P("tok"), P(), P(), P())
    out_specs = (P("tok"), P("tok"))
    return jax.shard_map(body, mesh=mesh, in_specs=in_specs, out_specs=out_specs, check_vma=False)
```

profile of v0, /device:TPU:1, one launch (start us, length us, event | category | flops | bytes accessed | tf_op | source)
XLA Modules:
  0.0 215.5 jit_solution(13861891363892837926)
XLA Ops:
  7.2 0.0 copy-start
  7.2 0.0 all-gather.3.cloned.1.call-start
  7.2 0.7 all-gather.3.cloned.1.call-update
  7.9 1.3 fusion.7
  11.2 0.8 dynamic-slice_bitcast_fusion
  11.9 42.7 %all-gather = bf16[32,1,1536]{2,1,0:T(2,128)(2,1)S(1)} all-gather(bf16[1,1,1536]{2,1,0:T(2,128)(2,1)S(1)} %dynamic-slice_bitcast_fusion), channel_id=1, replica_groups=mesh['tok'=32,'voc'=8] {'tok'}, dimensions={0}, use_global_device_ids=true | all-gather | bytes 101376 | tf_op jit(solution)/shard_map/all_gather | solution.py:61
  54.6 0.2 convert_element_type.12
  54.8 0.7 iota_compare_fusion.2
  55.5 0.1 fusion.4
  55.6 0.0 copy-done
  55.6 0.0 copy-start.3
  55.6 0.0 copy-start.1
  55.7 0.0 copy-start.2
  55.7 0.2 slice_convert_fusion
  55.8 0.3 multiply_reduce_fusion.1
  56.1 0.1 copy-done.3
  56.3 0.6 fusion.6
  56.9 0.0 copy-done.1
  57.0 108.5 %all-gather.3.cloned.1.call-done = bf16[1536,6144]{0,1:T(8,128)(2,1)} async-done(((bf16[1536,192]{0,1:T(8,128)(2,1)}), bf16[1536,6144]{0,1:T(8,128)(2,1)}) %all-gather.3.cloned.1.call-update) | async-done | bytes 18874384 | tf_op jit(solution)/shard_map/all_gather | solution.py:83
  165.4 0.0 copy-done.2
  165.4 10.8 %fusion.10 = (f32[256]{0:T(256)S(1)}, f32[256,6144]{1,0:T(8,128)}) fusion(bf16[1536,6144]{0,1:T(8,128)(2,1)} %all-gather.3.cloned.1.call-done, f32[255,1536]{1,0:T(8,128)S(1)} %slice_convert_fusion, f32[1,1536]{1,0:T(1,128)S(1)} %broadcast_in_dim.57, f32[1536]{0:T(1024)S(1)} %copy-done.2, f32[256]{0:T(256)S(1)} %add_rsqrt_fusion), kind=kOutput, calls=%fused_computation.42 | convolution fusion | flops 4834983936 | bytes 26746880 | tf_op jit(solution)/shard_map/while/body/eval_jaxpr/dot_general | solution.py:35
  176.3 12.8 %pmax.7 = f32[256]{0:T(256)S(1)} all-reduce(f32[256]{0:T(256)S(1)} %broadcast_maximum_fusion), channel_id=1, replica_groups=mesh['tok'=32,'voc'=8] {'voc'}, use_global_device_ids=true, to_apply=%region_8.9 | all-reduce | flops 256 | bytes 2048 | tf_op jit(solution)/shard_map/pmax | solution.py:85
  189.1 4.2 %multiply_reduce_fusion = (f32[256]{0:T(256)S(1)}, f32[256]{0:T(256)S(1)}, f32[256]{0:T(256)S(1)}) fusion(f32[256,6144]{1,0:T(8,128)} %get-tuple-element.42, f32[256]{0:T(256)S(1)} %get-tuple-element.41, s32[256]{0:T(256)S(1)} %compare_select_fusion.1), kind=kLoop, calls=%fused_computation | loop fusion | flops 11009280 | bytes 6296576 | tf_op jit(solution)/shard_map/while/body/eval_jaxpr/reduce_sum | solution.py:39
  193.2 14.2 %all-reduce = (f32[256]{0:T(256)S(1)}, f32[256]{0:T(256)S(1)}, f32[256]{0:T(256)S(1)}) all-reduce(f32[256]{0:T(256)S(1)} %get-tuple-element.22, f32[256]{0:T(256)S(1)} %get-tuple-element.40, f32[256]{0:T(256)S(1)} %get-tuple-element.39), channel_id=1, replica_groups=mesh['tok'=32,'voc'=8] {'voc'}, use_global_device_ids=true, to_apply=%region_6.7 | all-reduce | flops 768 | bytes 6144 | tf_op jit(solution)/shard_map/psum | solution.py:87
  207.4 1.2 subtract_select_fusion
  (5 shorter events, 0.1 us)
Async XLA Ops:
  7.2 48.5 %copy-start = (bf16[256,1536]{1,0:T(8,128)(2,1)S(1)}, bf16[256,1536]{1,0:T(8,128)(2,1)}, u32[]{:S(2)}) copy-start(bf16[256,1536]{1,0:T(8,128)(2,1)} %param.7) | copy-start | bytes 2359300
  7.2 158.2 %all-gather.3.cloned.1.call-start = ((), (), s32[]{:S(2)}) async-start(), calls=%async_computation | async-start | bytes 19464192 | tf_op jit(solution)/shard_map/all_gather | solution.py:83
  55.6 0.7 copy-start.3
  55.6 1.3 copy-start.1
  55.7 109.8 %copy-start.2 = (f32[1536]{0:T(1024)S(1)}, f32[1536]{0:T(1024)}, u32[]{:S(2)}) copy-start(f32[1536]{0:T(1024)} %param.8) | copy-start | bytes 18436
Sparse Core Ops, SparseCore 0:
  10.6 154.7 all-gather.2
where the time goes:
time: 216 us; the launch traced here: 215 us
  waiting for transfers between devices  109 us (50%)
  blocking collectives  69.7 us (32%)
  between operations  16.1 us (7%)
  matrix products  10.8 us (5%)
  other arithmetic  8.77 us (4%)
    all_gather x1, waiting for transfers between devices, body(): lax.all_gather(head_weight, 'tok', axis=1, tiled=True)  108 us
    all_gather x1, blocking collectives, body(): incoming = lax.all_gather(outgoing, 'tok', axis=0, tiled=True)  42.7 us
    psum x1, blocking collectives, body(): lax.psum((totals * factor, moments * factor, picked), 'voc')  14.2 us
    pmax x1, blocking collectives, body(): largest = lax.pmax(maxima, 'voc')  12.8 us
    dot_general x1, matrix products, score_block(): logits = jnp.dot(state_rows, columns, preferred_element_type=jnp.float32)  10.8 us
  transfers between devices with their start and end apart: 1, of which 1 were waited for; matrix products, arithmetic and copies ran while one was open for 2% of the time, Pallas kernels for 0%

commit v1 on v0

--- a/solution.py
+++ b/solution.py
@@ -4,6 +4,9 @@
 from jax.sharding import PartitionSpec as P
 
 epsilon = 1e-05
+get_points = lambda frame: jnp.concatenate(
+    lax.all_to_all(jnp.stack(lax.psum(1, "tok") * [frame]), "tok", 0, 0), axis=1
+)
 
 
 def select_entry(table, wanted):
@@ -79,8 +82,7 @@
     zeroes = jnp.zeros((row_count,), jnp.float32)
     initial = (jnp.full((row_count,), -1e30, jnp.float32), zeroes, zeroes, zeroes)
     maxima, totals, moments, picked = combine(
-        initial,
-        block_stats(normed, lax.all_gather(head_weight, "tok", axis=1, tiled=True), target_col),
+        initial, block_stats(normed, get_points(head_weight), target_col)
     )
     largest = lax.pmax(maxima, "voc")
     factor = jnp.exp(maxima - largest)

time: 216 us -> 559 us (2.59)
  blocking collectives: 69.7 us -> 517 us
  waiting for transfers between devices: 109 us -> 0.01 us
  between operations: 16.1 us -> 2.71 us
  starting transfers between devices: 0.04 us -> 12.3 us
  local copies, waits for them, and re-layouts: 0.93 us -> 7.82 us
    all_gather x1, blocking collectives: 42.7 us -> 482 us  [body(): incoming = lax.all_gather(outgoing, 'tok', axis=0, tiled=True)]
    all_gather x1 -> x0, waiting for transfers between devices: 108 us -> none  [body(): lax.all_gather(head_weight, 'tok', axis=1, tiled=True)]
    all_to_all x0 -> x1, starting transfers between devices: none -> 12.3 us  [lax.all_to_all(jnp.stack(lax.psum(1, 'tok') * [frame]), 'tok', 0, 0)]
    pmax x1, blocking collectives: 12.8 us -> 22.3 us  [body(): largest = lax.pmax(maxima, 'voc')]
    another operation x0 -> x1, local copies, waits for them, and re-layouts: none -> 7.62 us  [jnp.stack(lax.psum(1, 'tok') * [frame])]
  transfers between devices with their start and end apart: 1 -> 1, of which waited for: 1 -> 0; matrix products, arithmetic and copies ran while one was open for 2% -> 0% of each run, Pallas kernels for 0% -> 0%
where the time goes in v1:
time: 559 us
  blocking collectives  517 us (92%)
  starting transfers between devices  12.3 us (2%)
  matrix products  10.9 us (2%)
  other arithmetic  8.1 us (1%)
  local copies, waits for them, and re-layouts  7.82 us (1%)
    all_gather x1, blocking collectives, body(): incoming = lax.all_gather(outgoing, 'tok', axis=0, tiled=True)  482 us
    pmax x1, blocking collectives, body(): largest = lax.pmax(maxima, 'voc')  22.3 us
    psum x1, blocking collectives, body(): lax.psum((totals * factor, moments * factor, picked), 'voc')  12.4 us
    all_to_all x1, starting transfers between devices, lax.all_to_all(jnp.stack(lax.psum(1, 'tok') * [frame]), 'tok', 0, 0)  12.3 us
  transfers between devices with their start and end apart: 1, of which 0 were waited for; matrix products, arithmetic and copies ran while one was open for 0% of the time, Pallas kernels for 0%

profile of v1, /device:TPU:1, one launch (start us, length us, event | category | flops | bytes accessed | tf_op | source)
XLA Modules:
  0.0 558.8 jit_solution(10724298611261157223)
XLA Ops:
  0.6 7.6 %stack.2 = bf16[32,1536,192]{1,2,0:T(8,128)(2,1)} broadcast(bf16[1536,192]{0,1:T(8,128)(2,1)} %param.9), dimensions={1,2} | broadcast | bytes 19464192 | tf_op jit(solution)/shard_map/stack | solution.py:8
  8.2 0.0 copy-start.2
  8.3 0.0 copy-start.3
  8.3 0.0 copy-start
  8.3 12.3 %all-to-all-start = ((bf16[32,1536,192]{1,2,0:T(8,128)(2,1)}), bf16[32,1536,192]{1,2,0:T(8,128)(2,1)}, u32[]{:S(2)}, u32[]{:S(2)}) async-start(bf16[32,1536,192]{1,2,0:T(8,128)(2,1)} %stack.2), calls=%async_computation | async-start | bytes 37748736 | tf_op jit(solution)/shard_map/all_to_all | solution.py:8
  20.6 0.0 copy-done.2
  20.6 0.0 copy-done.3
  20.6 0.6 fusion.7
  23.2 0.0 copy-done
  23.2 482.2 %all-gather = bf16[32,1,1536]{2,1,0:T(2,128)(2,1)S(1)} all-gather(bf16[1,1,1536]{2,1,0:T(2,128)(2,1)S(1)} %dynamic-slice_bitcast_fusion), channel_id=1, replica_groups=mesh['tok'=32,'voc'=8] {'tok'}, dimensions={0}, use_global_device_ids=true | all-gather | bytes 101376 | tf_op jit(solution)/shard_map/all_gather | solution.py:64
  505.4 0.2 convert_element_type.12
  505.7 0.7 iota_compare_fusion.2
  506.3 0.1 fusion.4
  506.4 0.0 copy-start.5
  506.4 0.0 copy-start.1
  506.5 0.0 copy-start.4
  506.5 0.2 slice_convert_fusion
  506.7 0.3 multiply_reduce_fusion.1
  506.9 0.1 copy-done.5
  507.1 0.6 fusion.6
  507.7 0.0 copy-done.1
  507.8 0.0 all-to-all-done
  507.8 0.0 copy-done.4
  507.8 10.9 %fusion.10 = (f32[256]{0:T(256)S(1)}, f32[256,6144]{1,0:T(8,128)}) fusion(bf16[1536,6144]{0,1:T(8,128)(2,1)} %bitcast.2, f32[255,1536]{1,0:T(8,128)S(1)} %slice_convert_fusion, f32[1,1536]{1,0:T(1,128)S(1)} %broadcast_in_dim.57, f32[1536]{0:T(1024)S(1)} %copy-done.4, f32[256]{0:T(256)S(1)} %add_rsqrt_fusion), kind=kOutput, calls=%fused_computation.42 | convolution fusion | flops 4834983936 | bytes 26746880 | tf_op jit(solution)/shard_map/while/body/eval_jaxpr/dot_general | solution.py:38
  518.7 22.3 %pmax.7 = f32[256]{0:T(256)S(1)} all-reduce(f32[256]{0:T(256)S(1)} %broadcast_maximum_fusion), channel_id=1, replica_groups=mesh['tok'=32,'voc'=8] {'voc'}, use_global_device_ids=true, to_apply=%region_8.9 | all-reduce | flops 256 | bytes 2048 | tf_op jit(solution)/shard_map/pmax | solution.py:87
  541.0 4.2 multiply_reduce_fusion
  545.1 12.4 %all-reduce = (f32[256]{0:T(256)S(1)}, f32[256]{0:T(256)S(1)}, f32[256]{0:T(256)S(1)}) all-reduce(f32[256]{0:T(256)S(1)} %get-tuple-element.22, f32[256]{0:T(256)S(1)} %get-tuple-element.40, f32[256]{0:T(256)S(1)} %get-tuple-element.39), channel_id=1, replica_groups=mesh['tok'=32,'voc'=8] {'voc'}, use_global_device_ids=true, to_apply=%region_6.7 | all-reduce | flops 768 | bytes 6144 | tf_op jit(solution)/shard_map/psum | solution.py:89
  557.6 1.2 subtract_select_fusion
  (6 shorter events, 0.1 us)
Async XLA Ops:
  8.2 12.3 %copy-start.2 = (s32[32]{0:T(128)S(1)}, s32[32]{0:T(128)}, u32[]{:S(2)}) copy-start(s32[32]{0:T(128)} %param.12) | copy-start | bytes 388
  8.3 12.3 %copy-start.3 = (s32[32]{0:T(128)S(1)}, s32[32]{0:T(128)}, u32[]{:S(2)}) copy-start(s32[32]{0:T(128)} %param.13) | copy-start | bytes 388
  8.3 14.9 %copy-start = (bf16[256,1536]{1,0:T(8,128)(2,1)S(1)}, bf16[256,1536]{1,0:T(8,128)(2,1)}, u32[]{:S(2)}) copy-start(bf16[256,1536]{1,0:T(8,128)(2,1)} %param.7) | copy-start | bytes 2359300
  8.3 499.5 %all-to-all-start = ((bf16[32,1536,192]{1,2,0:T(8,128)(2,1)}), bf16[32,1536,192]{1,2,0:T(8,128)(2,1)}, u32[]{:S(2)}, u32[]{:S(2)}) async-start(bf16[32,1536,192]{1,2,0:T(8,128)(2,1)} %stack.2), calls=%async_computation | async-start | bytes 37748736 | tf_op jit(solution)/shard_map/all_to_all | solution.py:8
  506.4 0.7 copy-start.5
  506.4 1.3 copy-start.1
  506.5 1.3 copy-start.4
